TPU v7x, 512 devices: a whole 4x8x8 slice. The times are simulated.
512 devices in a mesh: seq: 64 (over y, x, z_hi), tp: 8 (over z_lo, core).
Axes of the slice: x: 4, y: 8, z: 8 (z_hi: 2, z_lo: 4; z = z_hi * 4 + z_lo), core: 2. Of those that a mesh axis runs over, the one named last changes fastest.
Arguments:
- queries: bfloat16 [16384, 4096], P('seq', 'tp'), may hold values from -90 to 90
- key_rows: bfloat16 [16384, 4096], P('seq', 'tp'), may hold values from -4 to 4
- value_rows: bfloat16 [16384, 4096], P('seq', 'tp'), may hold values from -5 to 5
- residual: bfloat16 [16384, 4096], P('seq', 'tp'), may hold values from -1.5 to 1.5
- out_weight: bfloat16 [4096, 4096], P('tp', 'seq'), may hold values from -0.09375 to 0.09375
- norm_gain: float32 [4096], P('tp'), may hold values from 0.5 to 1.5
- norm_bias: float32 [4096], P('tp'), may hold values from -1 to 1
- global_list: int32 [2], replicated, may hold values from 0 to 1023
- random_device: int32 [1024, 3], P('seq'), may hold values from 0 to 63, all different within a row; in each aligned block of 16 rows (0 to 15, 16 to 31, ...) at most 2 rows name the same one
- random_offset: int32 [1024, 3], P('seq'), may hold values from 0 to 15
- drop_seed: int32 [1], replicated, may hold values from 0 to 65535
- drop_offsets: int32 [1024], P('seq'), may hold values from 0 to 8388607
Outputs:
- encoded: bfloat16 [16384, 4096], P('seq', 'tp')
Inputs may be any that keep to these rules, and one draw needn't show every extreme that they name: `random_device`: each row names 3 different indices; among the 16 rows of one index of seq no index is named more than 2 times.
All inputs are finite; a program needn't handle non-finite values.
Results may differ from a plain program's by a relative error of at most 0.013.
Values may be sent and summed in bfloat16 or wider, within the bound.
No kernel may reach another device: no remote copies, remote signals or barrier semaphores. Data moves between devices by JAX's collectives and lax.ppermute only.
A program may use at most 64 MiB of HBM per device.

v0:
```python
import jax
import jax.numpy as jnp
from jax import lax
from jax.sharding import PartitionSpec as P

D = 4096
DH = 128
BLOCK = 16


def padded_2(x, sides, width):
    for axis, dim in sides:
        devices, length = (lax.axis_size(axis), x.shape[dim])
        up = [(i, (i + 1) % devices) for i in range(devices)]
        down = [(j, i) for i, j in up]
        last = lax.slice_in_dim(x, length - width, length, axis=dim)
        first = lax.slice_in_dim(x, 0, width, axis=dim)
        before = lax.ppermute(last, axis, up)
        after = lax.ppermute(first, axis, down)
        x = jnp.concatenate([before, x, after], axis=dim)
    return x


def broadcast(value, axis, source):
    kept = jnp.where(lax.axis_index(axis) == source, value, 0).astype(value.dtype)
    return lax.psum(kept, axis)


def mix_bits(counter, seed_value):
    hashed = counter + seed_value * 1000003
    for rounds in range(2):
        hashed = jnp.bitwise_xor(hashed, lax.shift_right_logical(hashed, jnp.int32(16)))
        hashed = hashed * 73244475
    hashed = jnp.bitwise_xor(hashed, lax.shift_right_logical(hashed, jnp.int32(16)))
    return hashed


def keep_table(counter, seed_value):
    hashed = mix_bits(counter, seed_value)
    kept = jnp.bitwise_and(hashed, 1023) >= 102
    return jnp.where(kept, jnp.float32(1024.0 / 922.0), jnp.float32(0.0))


def on_device(
    queries,
    key_rows,
    value_rows,
    residual,
    out_weight,
    norm_gain,
    norm_bias,
    global_list,
    random_device,
    random_offset,
    drop_seed,
    drop_offsets,
):
    row_count, width_here = queries.shape
    heads_here = width_here // DH
    block_count = row_count // BLOCK
    seq_count = lax.axis_size("seq")
    paired = jnp.concatenate([key_rows, value_rows], axis=1).reshape(
        block_count, BLOCK, 2 * width_here
    )
    padded = padded_2(paired, (("seq", 0),), 1)
    window = jnp.stack(
        [padded[0:block_count], padded[1 : block_count + 1], padded[2 : block_count + 2]], axis=1
    )
    glob_count = global_list.shape[0]
    fetched = []
    for which in range(glob_count):
        wanted_block = global_list[which]
        local_block = jnp.take(paired, wanted_block % block_count, axis=0)
        fetched.append(broadcast(local_block, "seq", wanted_block // block_count))
    glob_blocks = jnp.stack(fetched, axis=0)
    glob_blocks = jnp.broadcast_to(glob_blocks[None], (block_count,) + glob_blocks.shape)
    rand_count = random_device.shape[1]
    request_count = block_count * rand_count
    target = random_device.reshape(request_count)
    wanted = random_offset.reshape(request_count)
    request_rank = jnp.arange(request_count, dtype=jnp.int32)
    same_dest = target[:, None] == target[None, :]
    earlier = request_rank[None, :] < request_rank[:, None]
    slot_index = jnp.sum(jnp.logical_and(same_dest, earlier), axis=1)
    capacity = max(2, -(-request_count // seq_count))
    dest_ids = jnp.arange(seq_count, dtype=jnp.int32)
    slot_ids = jnp.arange(capacity, dtype=jnp.int32)
    matched = jnp.logical_and(
        target[None, None, :] == dest_ids[:, None, None],
        slot_index[None, None, :] == slot_ids[None, :, None],
    )
    request_table = jnp.sum(jnp.where(matched, wanted[None, None, :], 0), axis=2)
    picked = jnp.take(
        paired,
        lax.all_to_all(request_table, "seq", split_axis=0, concat_axis=0, tiled=True),
        axis=0,
    )
    replies = lax.all_to_all(picked, "seq", split_axis=0, concat_axis=0, tiled=True)
    flat_replies = replies.reshape(seq_count * capacity, BLOCK, 2 * width_here)
    chosen = jnp.take(flat_replies, target * capacity + slot_index, axis=0)
    chosen = chosen.reshape(block_count, rand_count, BLOCK, 2 * width_here)
    all_keys = jnp.concatenate([window, glob_blocks, chosen], axis=1)
    key_total = all_keys.shape[1] * BLOCK
    all_keys = all_keys.reshape(block_count, key_total, 2 * width_here)
    key_heads = all_keys[:, :, :width_here].reshape(block_count, key_total, heads_here, DH)
    value_heads = all_keys[:, :, width_here:].reshape(block_count, key_total, heads_here, DH)
    query_heads = queries.reshape(block_count, BLOCK, heads_here, DH)
    score_scale = jnp.float32(1.0 / DH**0.5)
    scores = (
        jnp.einsum("bqhd,bkhd->bhqk", query_heads, key_heads, preferred_element_type=jnp.float32)
        * score_scale
    )
    top_score = jnp.max(scores, axis=-1, keepdims=True)
    expo = jnp.exp(scores - top_score)
    attn_probs = (expo / jnp.sum(expo, axis=-1, keepdims=True)).astype(jnp.bfloat16)
    context = jnp.einsum(
        "bhqk,bkhd->bqhd", attn_probs, value_heads, preferred_element_type=jnp.float32
    )
    context = context.astype(jnp.bfloat16).reshape(row_count, width_here)
    partial_terms = jnp.dot(
        context,
        lax.all_gather(out_weight, "seq", axis=1, tiled=True),
        preferred_element_type=jnp.float32,
    )
    attended = lax.psum_scatter(
        partial_terms.astype(jnp.bfloat16), "tp", scatter_dimension=1, tiled=True
    ).astype(jnp.float32)
    cols_here = attended.shape[1]
    first_col = lax.axis_index("tp") * cols_here
    inner = jnp.arange(BLOCK, dtype=jnp.int32)
    columns = first_col + jnp.arange(cols_here, dtype=jnp.int32)
    counter = drop_offsets[:, None, None] + inner[None, :, None] * D + columns[None, None, :]
    keep_factor = keep_table(counter, drop_seed[0]).reshape(row_count, cols_here)
    summed_rows = residual.astype(jnp.float32) + keep_factor * attended
    row_total = lax.psum(jnp.sum(summed_rows, axis=1), "tp")
    row_mean = row_total / D
    centered = summed_rows - row_mean[:, None]
    spread = lax.psum(jnp.sum(centered * centered, axis=1), "tp")
    row_var = spread / D
    encoded = (
        centered * lax.rsqrt(row_var + 1e-05)[:, None] * norm_gain[None, :] + norm_bias[None, :]
    )
    return encoded.astype(jnp.bfloat16)


def solution(mesh):
    placed = (
        P("seq", "tp"),
        P("seq", "tp"),
        P("seq", "tp"),
        P("seq", "tp"),
        P("tp", "seq"),
        P("tp"),
        P("tp"),
        P(),
        P("seq", None),
        P("seq", None),
        P(),
        P("seq"),
    )
    return jax.shard_map(
        on_device, mesh=mesh, in_specs=placed, out_specs=P("seq", "tp"), check_vma=False
    )
```

profile of v0, /device:TPU:1, one launch (start us, length us, event | category | flops | bytes accessed | tf_op | source)
XLA Modules:
  0.0 1136.7 jit_solution(4310646254590320187)
XLA Ops:
  6.5 0.8 copy.68
  7.7 0.8 copy.70
  8.6 0.7 copy.71
  9.3 19.6 %all-to-all-start = ((s32[64,1,2]{2,1,0:T(1,128)}), s32[64,1,2]{2,1,0:T(1,128)S(1)}, u32[]{:S(2)}, u32[]{:S(2)}) async-start(s32[64,1,2]{2,1,0:T(1,128)} %copy.71), calls=%async_computation | async-start | bytes 65536 | tf_op jit(solution)/shard_map/all_to_all | solution.py:95
  28.9 1.0 constant_dynamic-update-slice_fusion.1
  29.9 1.0 constant_dynamic-update-slice_fusion
  30.9 11.2 all-to-all-done
  42.5 2.7 gather_fusion
  45.2 4.6 broadcast_select_fusion
  49.9 5.8 all-to-all-start.1
  63.3 6.6 collective-permute-start
  69.9 6.8 collective-permute-start.1
  77.0 73.8 %collective-permute-done = bf16[1,16,1024]{2,1,0:T(8,128)(2,1)S(1)} collective-permute-done((bf16[1,16,1024]{2,1,0:T(8,128)(2,1)S(1)}, bf16[1,16,1024]{2,1,0:T(8,128)(2,1)S(1)}, u32[]{:S(2)}, u32[]{:S(2)}) %collective-permute-start) | collective-permute-done | bytes 32800 | tf_op jit(solution)/shard_map/ppermute | solution.py:18
  150.8 0.8 fusion.12
  151.7 0.8 constant_dynamic-update-slice_fusion.2
  152.5 0.8 fusion.10
  153.4 702.0 %all-reduce.3.cloned.1.call-done = (bf16[1,16,1024]{2,1,0:T(8,128)(2,1)}, bf16[1,16,1024]{2,1,0:T(8,128)(2,1)}) async-done(((bf16[1,16,1024]{2,1,0:T(8,128)(2,1)}, bf16[1,16,1024]{2,1,0:T(8,128)(2,1)}), (bf16[1,16,1024]{2,1,0:T(8,128)(2,1)}, bf16[1,16,1024]{2,1,0:T(8,128)(2,1)})) %all-reduce.3.cloned.1.call-update) | async-done | bytes 65552 | tf_op jit(solution)/shard_map/psum | solution.py:26
  855.4 0.8 pad_maximum_fusion.2
  856.2 1.1 broadcast_dynamic-update-slice_fusion
  857.3 2.8 gather_fusion.1
  860.1 1.5 select_dynamic-update-slice_fusion
  861.6 4.6 fusion.23
  866.3 3.0 copy.80
  869.3 3.9 copy.79
  874.3 3.4 fusion.4
  877.8 175.0 %all-gather.2.cloned.1.call-done = bf16[512,4096]{0,1:T(8,128)(2,1)} async-done(((bf16[512,64]{0,1:T(8,128)(2,1)}), bf16[512,4096]{0,1:T(8,128)(2,1)}) %all-gather.2.cloned.1.call-update) | async-done | bytes 4194320 | tf_op jit(solution)/shard_map/all_gather | solution.py:122
  1052.8 4.8 convolution_convert_fusion
  1058.6 38.0 %reduce-scatter.2.cloned.1.call-done = bf16[256,512]{1,0:T(8,128)(2,1)} async-done(((bf16[256,4096]{1,0:T(8,128)(2,1)}), bf16[256,512]{1,0:T(8,128)(2,1)}) %reduce-scatter.2.cloned.1.call-update) | async-done | bytes 262160 | tf_op jit(solution)/shard_map/reduce_scatter | solution.py:125
  1096.6 1.4 fusion.22
  1098.1 16.2 %psum.30 = f32[256]{0:T(256)S(1)} all-reduce(f32[256]{0:T(256)S(1)} %get-tuple-element.19), channel_id=1, replica_groups=mesh['seq'=64,'tp'=8] {'tp'}, use_global_device_ids=true, to_apply=%region_8.10 | all-reduce | flops 256 | bytes 2048 | tf_op jit(solution)/shard_map/psum | solution.py:135
  1114.5 14.8 %psum.31 = f32[256]{0:T(256)S(1)} all-reduce(f32[256]{0:T(256)S(1)} %multiply_reduce_fusion), channel_id=1, replica_groups=mesh['seq'=64,'tp'=8] {'tp'}, use_global_device_ids=true, to_apply=%region_10.12 | all-reduce | flops 256 | bytes 2048 | tf_op jit(solution)/shard_map/psum | solution.py:138
  1129.3 0.9 add_convert_fusion
  (56 shorter events, 5.1 us)
Async XLA Ops:
  9.3 32.7 %all-to-all-start = ((s32[64,1,2]{2,1,0:T(1,128)}), s32[64,1,2]{2,1,0:T(1,128)S(1)}, u32[]{:S(2)}, u32[]{:S(2)}) async-start(s32[64,1,2]{2,1,0:T(1,128)} %copy.71), calls=%async_computation | async-start | bytes 65536 | tf_op jit(solution)/shard_map/all_to_all | solution.py:95
  49.9 5.9 copy-start.4
  49.9 27.1 %copy-start = (bf16[256,512]{1,0:T(8,128)(2,1)S(1)}, bf16[256,512]{1,0:T(8,128)(2,1)}, u32[]{:S(2)}) copy-start(bf16[256,512]{1,0:T(8,128)(2,1)} %param.14) | copy-start | bytes 786436
  49.9 807.4 %all-to-all-start.1 = ((bf16[64,2,16,1024]{3,2,1,0:T(8,128)(2,1)}), bf16[64,2,16,1024]{3,2,1,0:T(8,128)(2,1)}, u32[]{:S(2)}, u32[]{:S(2)}) async-start(bf16[64,2,16,1024]{3,2,1,0:T(8,128)(2,1)} %broadcast_select_fusion), calls=%async_computation.1 | async-start | bytes 8388608 | tf_op jit(solution)/shard_map/all_to_all | solution.py:98
  55.7 799.7 %all-reduce.3.cloned.1.call-start = ((), (), s32[]{:S(2)}) async-start(), calls=%async_computation.5 | async-start | bytes 131072 | tf_op jit(solution)/shard_map/psum | solution.py:26
  62.5 990.3 %all-gather.2.cloned.1.call-start = ((), (), s32[]{:S(2)}) async-start(), calls=%async_computation.3 | async-start | bytes 4259840 | tf_op jit(solution)/shard_map/all_gather | solution.py:122
  63.2 1033.4 %reduce-scatter.2.cloned.1.call-start = ((), (), s32[]{:S(2)}) async-start(), calls=%async_computation.4 | async-start | bytes 2359296 | tf_op jit(solution)/shard_map/reduce_scatter | solution.py:125
  63.3 87.6 %collective-permute-start = (bf16[1,16,1024]{2,1,0:T(8,128)(2,1)S(1)}, bf16[1,16,1024]{2,1,0:T(8,128)(2,1)S(1)}, u32[]{:S(2)}, u32[]{:S(2)}) collective-permute-start(bf16[1,16,1024]{2,1,0:T(8,128)(2,1)S(1)} %get-tuple-element.26), channel_id=1, source_target_pairs={{0,8},{8,16},{16,24},{24,32},{32,40},{40,48},{48,56},{56,64},{64,7... | collective-permute-start | bytes 98312 | tf_op jit(solution)/shard_map/ppermute | solution.py:18
  69.9 82.6 %collective-permute-start.1 = (bf16[1,16,1024]{2,1,0:T(8,128)(2,1)S(1)}, bf16[1,16,1024]{2,1,0:T(8,128)(2,1)S(1)}, u32[]{:S(2)}, u32[]{:S(2)}) collective-permute-start(bf16[1,16,1024]{2,1,0:T(8,128)(2,1)S(1)} %get-tuple-element.25), channel_id=1, source_target_pairs={{8,0},{16,8},{24,16},{32,24},{40,32},{48,40},{56,48},{64,56},{72,6... | collective-permute-start | bytes 98312 | tf_op jit(solution)/shard_map/ppermute | solution.py:19
  1052.8 5.0 copy-start.5
  1052.8 43.9 %copy-start.1 = (bf16[256,512]{1,0:T(8,128)(2,1)S(1)}, bf16[256,512]{1,0:T(8,128)(2,1)}, u32[]{:S(2)}) copy-start(bf16[256,512]{1,0:T(8,128)(2,1)} %param.17) | copy-start | bytes 786436
  1052.8 76.6 %copy-start.2 = (f32[512]{0:T(512)S(1)}, f32[512]{0:T(512)}, u32[]{:S(2)}) copy-start(f32[512]{0:T(512)} %param.20) | copy-start | bytes 6148
  1052.8 76.6 %copy-start.3 = (f32[512]{0:T(512)S(1)}, f32[512]{0:T(512)}, u32[]{:S(2)}) copy-start(f32[512]{0:T(512)} %param.19) | copy-start | bytes 6148
Sparse Core Ops, SparseCore 0:
  62.6 792.7 all-reduce.2
  860.7 191.9 all-gather.1
  1057.8 38.8 reduce-scatter.1
where the time goes:
time: 1140 us
  waiting for transfers between devices  1000 us (88%)
  starting transfers between devices  38.9 us (3%)
  blocking collectives  31.1 us (3%)
  local copies, waits for them, and re-layouts  25.2 us (2%)
  between operations  19.4 us (2%)
  other arithmetic  12.5 us (1%)
    psum x1, waiting for transfers between devices, broadcast(): return lax.psum(kept, axis)  702 us
    all_gather x1, waiting for transfers between devices, on_device(): lax.all_gather(out_weight, 'seq', axis=1, tiled=True)  175 us
    ppermute x1, waiting for transfers between devices, padded_2(): before = lax.ppermute(last, axis, up)  73.8 us
    reduce_scatter x1, waiting for transfers between devices, on_device(): lax.psum_scatter(partial_terms.astype(jnp.bfloat16), 'tp', scatter_dimens...  38 us
  transfers between devices with their start and end apart: 7, of which 5 were waited for; matrix products, arithmetic and copies ran while one was open for 3% of the time, Pallas kernels for 0%

commit v1 on v0

--- a/solution.py
+++ b/solution.py
@@ -23,7 +23,7 @@
 
 def broadcast(value, axis, source):
     kept = jnp.where(lax.axis_index(axis) == source, value, 0).astype(value.dtype)
-    return lax.psum(kept, axis)
+    return jnp.sum(lax.all_gather(kept, axis), axis=0)
 
 
 def mix_bits(counter, seed_value):

time: 1140 us -> 613 us (0.54)
  waiting for transfers between devices: 1000 us -> 460 us
  blocking collectives: 31.1 us -> 63.6 us
  starting transfers between devices: 38.9 us -> 19.3 us
    psum x1 -> x0, waiting for transfers between devices: 702 us -> none  [broadcast(): return lax.psum(kept, axis)]
    all_gather x0 -> x2, waiting for transfers between devices: none -> 207 us  [broadcast(): return jnp.sum(lax.all_gather(kept, axis), axis=0)]
    all_gather x1, waiting for transfers between devices: 175 us -> 133 us  [on_device(): lax.all_gather(out_weight, 'seq', axis=1, tiled=True)]
    all_to_all x0 -> x1, blocking collectives: none -> 32.6 us  [on_device(): lax.all_to_all(request_table, 'seq', split_axis=0, concat_axis=0, tiled=T...]
    all_to_all x1 -> x0, starting transfers between devices: 19.6 us -> none  [on_device(): lax.all_to_all(request_table, 'seq', split_axis=0, concat_axis=0, tiled=T...]
  transfers between devices with their start and end apart: 7 -> 7, of which waited for: 5 -> 5; matrix products, arithmetic and copies ran while one was open for 3% -> 6% of each run, Pallas kernels for 0% -> 0%
where the time goes in v1:
time: 613 us; the launch traced here: 612 us
  waiting for transfers between devices  460 us (75%)
  blocking collectives  63.6 us (10%)
  local copies, waits for them, and re-layouts  25.4 us (4%)
  between operations  19.4 us (3%)
  starting transfers between devices  19.3 us (3%)
  other arithmetic  15.6 us (3%)
  matrix products  8.9 us (1%)
    all_gather x2, waiting for transfers between devices, broadcast(): return jnp.sum(lax.all_gather(kept, axis), axis=0)  207 us
    all_gather x1, waiting for transfers between devices, on_device(): lax.all_gather(out_weight, 'seq', axis=1, tiled=True)  133 us
    ppermute x1, waiting for transfers between devices, padded_2(): before = lax.ppermute(last, axis, up)  80.9 us
    reduce_scatter x1, waiting for transfers between devices, on_device(): lax.psum_scatter(partial_terms.astype(jnp.bfloat16), 'tp', scatter_dimens...  38 us
    all_to_all x1, blocking collectives, on_device(): lax.all_to_all(request_table, 'seq', split_axis=0, concat_axis=0, tiled=T...  32.6 us
    psum x1, blocking collectives, on_device(): row_total = lax.psum(jnp.sum(summed_rows, axis=1), 'tp')  16.2 us
    psum x1, blocking collectives, on_device(): spread = lax.psum(jnp.sum(centered * centered, axis=1), 'tp')  14.9 us
  transfers between devices with their start and end apart: 7, of which 5 were waited for; matrix products, arithmetic and copies ran while one was open for 6% of the time, Pallas kernels for 0%

profile of v1, /device:TPU:1, one launch (start us, length us, event | category | flops | bytes accessed | tf_op | source)
XLA Modules:
  0.0 612.5 jit_solution(10002710435305056970)
XLA Ops:
  6.5 1.4 fusion.22
  13.3 1.0 constant_dynamic-update-slice_fusion.1
  14.3 1.0 constant_dynamic-update-slice_fusion
  17.6 0.8 copy.69
  18.9 32.6 %all_to_all.20 = s32[64,1,2]{2,1,0:T(1,128)S(1)} all-to-all(s32[64,1,2]{2,1,0:T(1,128)S(1)} %copy.70), channel_id=1, replica_groups=mesh['seq'=64,'tp'=8] {'seq'}, dimensions={0} | all-to-all | bytes 1024 | tf_op jit(solution)/shard_map/all_to_all | solution.py:95
  51.8 2.7 gather_fusion
  54.7 4.6 broadcast_select_fusion
  59.3 5.8 all-to-all-start.1
  65.9 6.6 %collective-permute-start = (bf16[1,16,1024]{2,1,0:T(8,128)(2,1)S(1)}, bf16[1,16,1024]{2,1,0:T(8,128)(2,1)S(1)}, u32[]{:S(2)}, u32[]{:S(2)}) collective-permute-start(bf16[1,16,1024]{2,1,0:T(8,128)(2,1)S(1)} %get-tuple-element.24), channel_id=1, source_target_pairs={{0,8},{8,16},{16,24},{24,32},{32,40},{40,48},{48,56},{56,64},{64,7... | collective-permute-start | bytes 98312 | tf_op jit(solution)/shard_map/ppermute | solution.py:18
  72.6 6.8 %collective-permute-start.1 = (bf16[1,16,1024]{2,1,0:T(8,128)(2,1)S(1)}, bf16[1,16,1024]{2,1,0:T(8,128)(2,1)S(1)}, u32[]{:S(2)}, u32[]{:S(2)}) collective-permute-start(bf16[1,16,1024]{2,1,0:T(8,128)(2,1)S(1)} %get-tuple-element.23), channel_id=1, source_target_pairs={{8,0},{16,8},{24,16},{32,24},{40,32},{48,40},{56,48},{64,56},{72,6... | collective-permute-start | bytes 98312 | tf_op jit(solution)/shard_map/ppermute | solution.py:19
  79.7 80.9 %collective-permute-done = bf16[1,16,1024]{2,1,0:T(8,128)(2,1)S(1)} collective-permute-done((bf16[1,16,1024]{2,1,0:T(8,128)(2,1)S(1)}, bf16[1,16,1024]{2,1,0:T(8,128)(2,1)S(1)}, u32[]{:S(2)}, u32[]{:S(2)}) %collective-permute-start) | collective-permute-done | bytes 32800 | tf_op jit(solution)/shard_map/ppermute | solution.py:18
  160.6 0.8 fusion.12
  161.4 0.8 constant_dynamic-update-slice_fusion.2
  162.2 0.8 fusion.10
  163.1 72.1 %all-gather.8.cloned.1.call-done = bf16[1024,1024]{1,0:T(8,128)(2,1)} async-done(((bf16[16,1024]{1,0:T(8,128)(2,1)}), bf16[1024,1024]{1,0:T(8,128)(2,1)}) %all-gather.8.cloned.1.call-update) | async-done | bytes 2097168 | tf_op jit(solution)/shard_map/all_gather | solution.py:26
  235.2 1.9 reduce_sum.73
  237.1 134.9 %all-gather.10.cloned.1.call-done = bf16[1024,1024]{1,0:T(8,128)(2,1)} async-done(((bf16[16,1024]{1,0:T(8,128)(2,1)}), bf16[1024,1024]{1,0:T(8,128)(2,1)}) %all-gather.10.cloned.1.call-update) | async-done | bytes 2097168 | tf_op jit(solution)/shard_map/all_gather | solution.py:26
  372.0 1.9 reduce_sum.74
  374.0 1.1 broadcast_dynamic-update-slice_fusion
  375.1 2.8 gather_fusion.1
  378.0 1.5 select_dynamic-update-slice_fusion
  379.4 4.6 fusion.21
  384.1 3.0 copy.79
  387.1 3.9 copy.78
  392.1 3.4 fusion.4
  395.6 132.9 %all-gather.6.cloned.1.call-done = bf16[512,4096]{0,1:T(8,128)(2,1)} async-done(((bf16[512,64]{0,1:T(8,128)(2,1)}), bf16[512,4096]{0,1:T(8,128)(2,1)}) %all-gather.6.cloned.1.call-update) | async-done | bytes 4194320 | tf_op jit(solution)/shard_map/all_gather | solution.py:122
  528.6 4.9 convolution_convert_fusion
  534.4 38.0 %reduce-scatter.2.cloned.1.call-done = bf16[256,512]{1,0:T(8,128)(2,1)} async-done(((bf16[256,4096]{1,0:T(8,128)(2,1)}), bf16[256,512]{1,0:T(8,128)(2,1)}) %reduce-scatter.2.cloned.1.call-update) | async-done | bytes 262160 | tf_op jit(solution)/shard_map/reduce_scatter | solution.py:125
  572.4 1.4 fusion.20
  573.8 16.2 %psum.14 = f32[256]{0:T(256)S(1)} all-reduce(f32[256]{0:T(256)S(1)} %get-tuple-element.17), channel_id=1, replica_groups=mesh['seq'=64,'tp'=8] {'tp'}, use_global_device_ids=true, to_apply=%region_8.10 | all-reduce | flops 256 | bytes 2048 | tf_op jit(solution)/shard_map/psum | solution.py:135
  590.2 14.9 %psum.15 = f32[256]{0:T(256)S(1)} all-reduce(f32[256]{0:T(256)S(1)} %multiply_reduce_fusion), channel_id=1, replica_groups=mesh['seq'=64,'tp'=8] {'tp'}, use_global_device_ids=true, to_apply=%region_10.12 | all-reduce | flops 256 | bytes 2048 | tf_op jit(solution)/shard_map/psum | solution.py:138
  605.1 0.9 add_convert_fusion
  (58 shorter events, 6.0 us)
Async XLA Ops:
  6.5 228.6 %all-gather.8.cloned.1.call-start = ((), (), s32[]{:S(2)}) async-start(), calls=%async_computation.5 | async-start | bytes 2129920 | tf_op jit(solution)/shard_map/all_gather | solution.py:26
  16.0 356.1 %all-gather.10.cloned.1.call-start = ((), (), s32[]{:S(2)}) async-start(), calls=%async_computation.6 | async-start | bytes 2129920 | tf_op jit(solution)/shard_map/all_gather | solution.py:26
  59.3 20.3 %copy-start = (bf16[256,512]{1,0:T(8,128)(2,1)S(1)}, bf16[256,512]{1,0:T(8,128)(2,1)}, u32[]{:S(2)}) copy-start(bf16[256,512]{1,0:T(8,128)(2,1)} %param.14) | copy-start | bytes 786436
  59.3 315.8 %all-to-all-start.1 = ((bf16[64,2,16,1024]{3,2,1,0:T(8,128)(2,1)}), bf16[64,2,16,1024]{3,2,1,0:T(8,128)(2,1)}, u32[]{:S(2)}, u32[]{:S(2)}) async-start(bf16[64,2,16,1024]{3,2,1,0:T(8,128)(2,1)} %broadcast_select_fusion), calls=%async_computation.1 | async-start | bytes 8388608 | tf_op jit(solution)/shard_map/all_to_all | solution.py:98
  65.1 463.4 %all-gather.6.cloned.1.call-start = ((), (), s32[]{:S(2)}) async-start(), calls=%async_computation.3 | async-start | bytes 4259840 | tf_op jit(solution)/shard_map/all_gather | solution.py:122
  65.9 506.6 %reduce-scatter.2.cloned.1.call-start = ((), (), s32[]{:S(2)}) async-start(), calls=%async_computation.4 | async-start | bytes 2359296 | tf_op jit(solution)/shard_map/reduce_scatter | solution.py:125
  65.9 94.7 %collective-permute-start = (bf16[1,16,1024]{2,1,0:T(8,128)(2,1)S(1)}, bf16[1,16,1024]{2,1,0:T(8,128)(2,1)S(1)}, u32[]{:S(2)}, u32[]{:S(2)}) collective-permute-start(bf16[1,16,1024]{2,1,0:T(8,128)(2,1)S(1)} %get-tuple-element.24), channel_id=1, source_target_pairs={{0,8},{8,16},{16,24},{24,32},{32,40},{40,48},{48,56},{56,64},{64,7... | collective-permute-start | bytes 98312 | tf_op jit(solution)/shard_map/ppermute | solution.py:18
  72.6 89.7 %collective-permute-start.1 = (bf16[1,16,1024]{2,1,0:T(8,128)(2,1)S(1)}, bf16[1,16,1024]{2,1,0:T(8,128)(2,1)S(1)}, u32[]{:S(2)}, u32[]{:S(2)}) collective-permute-start(bf16[1,16,1024]{2,1,0:T(8,128)(2,1)S(1)} %get-tuple-element.23), channel_id=1, source_target_pairs={{8,0},{16,8},{24,16},{32,24},{40,32},{48,40},{56,48},{64,56},{72,6... | collective-permute-start | bytes 98312 | tf_op jit(solution)/shard_map/ppermute | solution.py:19
  528.5 5.0 copy-start.4
  528.6 43.9 %copy-start.1 = (bf16[256,512]{1,0:T(8,128)(2,1)S(1)}, bf16[256,512]{1,0:T(8,128)(2,1)}, u32[]{:S(2)}) copy-start(bf16[256,512]{1,0:T(8,128)(2,1)} %param.17) | copy-start | bytes 786436
  528.6 76.5 %copy-start.2 = (f32[512]{0:T(512)S(1)}, f32[512]{0:T(512)}, u32[]{:S(2)}) copy-start(f32[512]{0:T(512)} %param.20) | copy-start | bytes 6148
  528.6 76.5 %copy-start.3 = (f32[512]{0:T(512)S(1)}, f32[512]{0:T(512)}, u32[]{:S(2)}) copy-start(f32[512]{0:T(512)} %param.19) | copy-start | bytes 6148
Sparse Core Ops, SparseCore 0:
  16.1 219.0 all-gather.7
  239.7 132.3 all-gather.9
  376.6 151.9 all-gather.5
  533.6 38.8 reduce-scatter.1
